TPU v7x, 32 devices: a whole 2x2x4 slice. The times are simulated.
32 devices in a mesh: dom: 16 (over z, x, core), col: 2 (over y).
Axes of the slice: x: 2, y: 2, z: 4, core: 2. Of those that a mesh axis runs over, the one named last changes fastest.
Arguments:
- snapshots: bfloat16 [128, 3, 32768], P('col', None, 'dom'), may hold values from -30 to 30
- mass_tiles: bfloat16 [16, 3, 3, 32768], P(None, None, None, 'dom'), may hold values from -2 to 2
- tile_slot: int32 [15, 32768], P(None, 'dom'), may hold values from 0 to 3071
- send_up: int32 [8192], P('dom'), may hold values from 0 to 2047
- send_down: int32 [8192], P('dom'), may hold values from 0 to 2047
Outputs:
- mass_snap: bfloat16 [128, 3, 32768], P('col', None, 'dom')
- gram: float32 [128, 128], P(None, 'col')
Inputs may be any that keep to these rules, and one draw needn't show every extreme that they name: `tile_slot`: slots below 2048 are the partition's own nodes, the next 512 those received from the previous partition, the last 512 those from the next partition.
All inputs are finite; a program needn't handle non-finite values.
Results may differ from a plain program's by a relative error of at most 0.001.
Values may be sent and summed in bfloat16 or wider, within the bound.
No kernel may reach another device: no remote copies, remote signals or barrier semaphores. Data moves between devices by JAX's collectives and lax.ppermute only.
A program may use at most 64 MiB of HBM per device.

v0:
```python
import jax
import jax.numpy as jnp
from jax import lax
from jax.sharding import PartitionSpec as P


def shifted(value, axis, steps):
    count = lax.axis_size(axis)
    leading, last = (max(0, -steps), min(count, count - steps))
    return lax.ppermute(value, axis, [(source, source + steps) for source in range(leading, last)])


def couple(tiles, values):
    total_sum = tiles[None, :, 0, :].astype(jnp.float32) * values[:, None, 0, :].astype(jnp.float32)
    for in_comp in (1, 2):
        total_sum = total_sum + tiles[None, :, in_comp, :].astype(jnp.float32) * values[
            :, None, in_comp, :
        ].astype(jnp.float32)
    return total_sum


def apply_mass(local_snap, flat_ext, mass_tiles, tile_slot):
    snap_count = local_snap.shape[0]
    node_count = local_snap.shape[2]
    others = tile_slot.shape[0]
    total_sum = couple(mass_tiles[0], local_snap)
    gathered = jnp.take(flat_ext, tile_slot.reshape(-1), axis=1)
    gathered = gathered.reshape(snap_count, 3, others, node_count)
    for in_comp in (0, 1, 2):
        tile_part = jnp.transpose(mass_tiles[1:, :, in_comp, :], (1, 0, 2)).astype(jnp.float32)
        values = gathered[:, in_comp].astype(jnp.float32)
        total_sum = total_sum + jnp.sum(tile_part[None] * values[:, None], axis=2)
    return total_sum.astype(jnp.bfloat16)


def inner_products(left_rows, right_rows):
    left_flat = left_rows.reshape(left_rows.shape[0], -1)
    right_flat = right_rows.reshape(right_rows.shape[0], -1)
    return lax.dot_general(
        left_flat, right_flat, (((1,), (1,)), ((), ())), preferred_element_type=jnp.float32
    )


def body(snapshots, mass_tiles, tile_slot, send_up, send_down):
    snap_count = snapshots.shape[0]
    flat_local = snapshots.reshape(snap_count * 3, -1)
    to_upper = jnp.take(flat_local, send_up, axis=1)
    to_lower = jnp.take(flat_local, send_down, axis=1)
    from_lower = shifted(to_upper, "dom", 1)
    from_upper = shifted(to_lower, "dom", -1)
    flat_ext = jnp.concatenate([flat_local, from_lower, from_upper], axis=1)
    mass_snap = apply_mass(snapshots, flat_ext, mass_tiles, tile_slot)
    block_terms = inner_products(lax.all_gather(snapshots, "col", axis=0, tiled=True), mass_snap)
    summed_gram = lax.psum(block_terms, "dom")
    node_total = 3.0 * snapshots.shape[2] * lax.axis_size("dom")
    gram = summed_gram / node_total
    return (mass_snap, gram)


def solution(mesh):
    placed = (P("col", None, "dom"), P(None, None, None, "dom"), P(None, "dom"), P("dom"), P("dom"))
    return jax.shard_map(
        body,
        mesh=mesh,
        in_specs=placed,
        out_specs=(P("col", None, "dom"), P(None, "col")),
        check_vma=False,
    )
```

profile of v0, /device:TPU:0, one launch (start us, length us, event | category | flops | bytes accessed | tf_op | source)
XLA Modules:
  0.0 300.8 jit_solution(1382220188660814233)
XLA Ops:
  7.2 0.0 all-gather.2.cloned.1.call-start
  7.2 0.7 all-gather.2.cloned.1.call-update
  7.9 1.8 copy.30
  9.7 0.7 compare_select_fusion.3
  10.4 0.7 compare_and_fusion.2
  11.1 0.7 reshape.93
  11.8 0.5 copy.33
  12.3 2.0 gather_fusion.1
  14.3 0.8 select_bitcast_fusion.1
  15.2 2.4 collective-permute-start
  17.6 2.0 gather_fusion.2
  19.6 0.1 select_bitcast_fusion
  19.7 1.5 collective-permute-start.1
  21.2 1.1 convert_bitcast_fusion.2
  22.3 1.2 bitcast_convert_fusion.2
  23.6 0.1 copy.40
  23.8 0.1 compare_select_fusion
  24.0 0.1 slice_convert_fusion.2
  24.1 0.7 copy-done.10
  24.8 0.4 collective-permute-done.1
  25.2 1.2 pad_maximum_fusion
  26.5 120.6 %gather_fusion = bf16[30720,192]{1,0:T(8,128)(2,1)} fusion(bf16[192,3072]{0,1:T(8,128)(2,1)S(1)} %pad_maximum_fusion, s32[30720]{0:T(1024)S(1)} %broadcast_clamp_fusion), kind=kCustom, calls=%fused_computation.2 | custom fusion | bytes 23715840 | tf_op jit(solution)/shard_map/jit(_take)/gather | solution.py:27
  147.1 18.1 %copy.34 = bf16[192,30720]{1,0:T(8,128)(2,1)} copy(bf16[192,30720]{0,1:T(8,128)(2,1)} %bitcast.65) | data formatting | bytes 23592960 | tf_op jit(solution)/shard_map/jit(_take)/gather | solution.py:27
  165.1 17.4 %gather.10 = bf16[64,3,15,2048]{3,2,1,0:T(8,128)(2,1)} reshape(bf16[192,30720]{1,0:T(8,128)(2,1)} %copy.34) | data formatting | bytes 23592960 | tf_op jit(solution)/shard_map/jit(_take)/gather | solution.py:27
  182.6 21.2 %copy_select_fusion = bf16[64,3,15,2048]{3,0,2,1:T(8,128)(2,1)S(1)} fusion(bf16[64,3,15,2048]{3,2,1,0:T(8,128)(2,1)} %gather.10, pred[15,2048]{1,0:T(8,128)(4,1)S(1)} %compare_and_fusion), kind=kLoop, calls=%fused_computation.6 | loop fusion | flops 5898240 | bytes 23623680 | tf_op jit(solution)/shard_map/jit(_take)/select_n | solution.py:27
  203.8 9.2 %fusion.2 = (f32[64,15,2048]{2,0,1:T(8,128)}, f32[64,15,2048]{2,0,1:T(8,128)}, f32[64,15,2048]{2,0,1:T(8,128)}) fusion(bf16[64,3,15,2048]{3,0,2,1:T(8,128)(2,1)S(1)} %copy_select_fusion), kind=kLoop, calls=%fused_computation.12 | loop fusion | flops 5898240 | bytes 35389440 | tf_op jit(solution)/shard_map/mul | solution.py:32
  213.0 5.1 %multiply_reduce_fusion.2 = f32[64,3,2048]{2,0,1:T(8,128)S(1)} fusion(f32[64,15,2048]{2,0,1:T(8,128)} %get-tuple-element.3, f32[3,15,2048]{2,1,0:T(8,128)S(1)} %copy-done.5), kind=kLoop, calls=%fused_computation.5 | loop fusion | flops 11403264 | bytes 9805824 | tf_op jit(solution)/shard_map/reduce_sum | solution.py:32
  218.2 8.7 %multiply_reduce_fusion = (f32[64,3,2048]{2,0,1:T(8,128)S(1)}, f32[64,3,2048]{2,0,1:T(8,128)S(1)}) fusion(f32[64,15,2048]{2,0,1:T(8,128)} %get-tuple-element.4, f32[3,15,2048]{2,1,0:T(8,128)S(1)} %copy-done.6, f32[64,15,2048]{2,0,1:T(8,128)} %get-tuple-element.5, f32[3,15,2048]{2,1,0:T(8,128)S(1)} %copy-done.7), kind=kLoop, calls=%fused_computation.3 | loop fusion | flops 22806528 | bytes 19611648 | tf_op jit(solution)/shard_map/reduce_sum | solution.py:32
  226.9 0.7 add_convert_fusion
  227.6 2.3 convolution_bitcast_fusion
  230.0 63.3 %psum.7 = f32[128,64]{0,1:T(8,128)S(1)} all-reduce(f32[128,64]{0,1:T(8,128)S(1)} %convolution_bitcast_fusion), channel_id=1, replica_groups=mesh['dom'=16,'col'=2] {'dom'}, use_global_device_ids=true, to_apply=%region_3.5 | all-reduce | flops 8192 | bytes 65536 | tf_op jit(solution)/shard_map/psum | solution.py:54
  293.3 0.6 broadcast_multiply_fusion
  (35 shorter events, 0.3 us)
Async XLA Ops:
  7.2 220.5 %all-gather.2.cloned.1.call-start = ((), (), s32[]{:S(2)}) async-start(), calls=%async_computation | async-start | bytes 2359296 | tf_op jit(solution)/shard_map/all_gather | solution.py:53
  9.7 7.9 %copy-start.11 = (s32[512]{0:T(512)S(1)}, s32[512]{0:T(512)}, u32[]{:S(2)}) copy-start(s32[512]{0:T(512)} %param.11) | copy-start | bytes 6148
  11.8 9.4 %copy-start.8 = (bf16[16,3,3,2048]{3,0,2,1:T(8,128)(2,1)S(1)}, bf16[16,3,3,2048]{3,0,2,1:T(8,128)(2,1)}, u32[]{:S(2)}) copy-start(bf16[16,3,3,2048]{3,0,2,1:T(8,128)(2,1)} %param.8) | copy-start | bytes 1769476
  12.3 10.0 %copy-start = (bf16[64,3,2048]{2,0,1:T(8,128)(2,1)S(1)}, bf16[64,3,2048]{2,0,1:T(8,128)(2,1)}, u32[]{:S(2)}) copy-start(bf16[64,3,2048]{2,0,1:T(8,128)(2,1)} %param.7) | copy-start | bytes 2359300
  15.2 8.9 %collective-permute-start = (bf16[192,512]{0,1:T(8,128)(2,1)}, bf16[192,512]{0,1:T(8,128)(2,1)S(1)}, u32[]{:S(2)}, u32[]{:S(2)}) collective-permute-start(bf16[192,512]{0,1:T(8,128)(2,1)} %select_bitcast_fusion.1), channel_id=1, source_target_pairs={{0,2},{2,4},{4,6},{6,8},{8,10},{10,12},{12,14},{14,16},{16,18},{18... | collective-permute-start | bytes 589832 | tf_op jit(solution)/shard_map/ppermute | solution.py:10
  17.6 6.0 %copy-start.9 = (s32[15,2048]{1,0:T(8,128)S(1)}, s32[15,2048]{1,0:T(8,128)}, u32[]{:S(2)}) copy-start(s32[15,2048]{1,0:T(8,128)} %param.9) | copy-start | bytes 368644
  19.7 5.5 %collective-permute-start.1 = (bf16[192,512]{0,1:T(8,128)(2,1)S(1)}, bf16[192,512]{0,1:T(8,128)(2,1)S(1)}, u32[]{:S(2)}, u32[]{:S(2)}) collective-permute-start(bf16[192,512]{0,1:T(8,128)(2,1)S(1)} %select_bitcast_fusion), channel_id=1, source_target_pairs={{2,0},{4,2},{6,4},{8,6},{10,8},{12,10},{14,12},{16,14},{18,16},{20... | collective-permute-start | bytes 589832 | tf_op jit(solution)/shard_map/ppermute | solution.py:10
  24.1 0.7 copy-start.10
  203.8 9.2 %copy-start.5 = (f32[3,15,2048]{2,1,0:T(8,128)S(1)}, f32[3,15,2048]{2,1,0:T(8,128)}, u32[]{:S(2)}) copy-start(f32[3,15,2048]{2,1,0:T(8,128)} %get-tuple-element.9) | copy-start | bytes 1105924
  213.0 5.1 %copy-start.6 = (f32[3,15,2048]{2,1,0:T(8,128)S(1)}, f32[3,15,2048]{2,1,0:T(8,128)}, u32[]{:S(2)}) copy-start(f32[3,15,2048]{2,1,0:T(8,128)} %get-tuple-element.10) | copy-start | bytes 1105924
  213.0 5.1 %copy-start.7 = (f32[3,15,2048]{2,1,0:T(8,128)S(1)}, f32[3,15,2048]{2,1,0:T(8,128)}, u32[]{:S(2)}) copy-start(f32[3,15,2048]{2,1,0:T(8,128)} %get-tuple-element.11) | copy-start | bytes 1105924
  218.1 8.7 %copy-start.2 = (f32[64,2048]{1,0:T(8,128)S(1)}, f32[64,2048]{1,0:T(8,128)}, u32[]{:S(2)}) copy-start(f32[64,2048]{1,0:T(8,128)} %get-tuple-element.6) | copy-start | bytes 1572868
  218.1 8.7 %copy-start.3 = (f32[64,2048]{1,0:T(8,128)S(1)}, f32[64,2048]{1,0:T(8,128)}, u32[]{:S(2)}) copy-start(f32[64,2048]{1,0:T(8,128)} %get-tuple-element.7) | copy-start | bytes 1572868
  218.1 8.7 %copy-start.4 = (f32[64,2048]{1,0:T(8,128)S(1)}, f32[64,2048]{1,0:T(8,128)}, u32[]{:S(2)}) copy-start(f32[64,2048]{1,0:T(8,128)} %get-tuple-element.8) | copy-start | bytes 1572868
  227.6 66.3 %copy-start.1 = (bf16[64,3,2048]{2,0,1:T(8,128)(2,1)}, bf16[64,3,2048]{2,0,1:T(8,128)(2,1)S(1)}, u32[]{:S(2)}) copy-start(bf16[64,3,2048]{2,0,1:T(8,128)(2,1)S(1)} %add_convert_fusion) | copy-start | bytes 2359300
Sparse Core Ops, SparseCore 0:
  9.5 29.8 all-gather.1
where the time goes:
time: 302 us; the launch traced here: 301 us
  local copies, waits for them, and re-layouts  164 us (54%)
  blocking collectives  63.3 us (21%)
  other arithmetic  51.7 us (17%)
  between operations  14.4 us (5%)
  starting transfers between devices  3.91 us (1%)
    gather x3, local copies, waits for them, and re-layouts, apply_mass(): gathered = jnp.take(flat_ext, tile_slot.reshape(-1), axis=1)  156 us
    psum x1, blocking collectives, body(): summed_gram = lax.psum(block_terms, 'dom')  63.3 us
    select_n x2, other arithmetic, apply_mass(): gathered = jnp.take(flat_ext, tile_slot.reshape(-1), axis=1)  21.3 us
    reduce_sum x2, other arithmetic, apply_mass(): total_sum = total_sum + jnp.sum(tile_part[None] * values[:, None], axis=2)  13.8 us
    mul x1, other arithmetic, apply_mass(): total_sum = total_sum + jnp.sum(tile_part[None] * values[:, None], axis=2)  9.23 us
  transfers between devices with their start and end apart: 3, of which 1 were waited for; matrix products, arithmetic and copies ran while one was open for 71% of the time, Pallas kernels for 0%

commit v1 on v0

--- a/solution.py
+++ b/solution.py
@@ -51,7 +51,7 @@
     flat_ext = jnp.concatenate([flat_local, from_lower, from_upper], axis=1)
     mass_snap = apply_mass(snapshots, flat_ext, mass_tiles, tile_slot)
     block_terms = inner_products(lax.all_gather(snapshots, "col", axis=0, tiled=True), mass_snap)
-    summed_gram = lax.psum(block_terms, "dom")
+    summed_gram = jnp.sum(lax.all_gather(block_terms, "dom"), axis=0)
     node_total = 3.0 * snapshots.shape[2] * lax.axis_size("dom")
     gram = summed_gram / node_total
     return (mass_snap, gram)

time: 302 us -> 265 us (0.88)
  blocking collectives: 63.3 us -> 26 us
    psum x1 -> x0, blocking collectives: 63.3 us -> none  [body(): summed_gram = lax.psum(block_terms, 'dom')]
    all_gather x0 -> x1, blocking collectives: none -> 26 us  [body(): summed_gram = jnp.sum(lax.all_gather(block_terms, 'dom'), axis=0)]
  transfers between devices with their start and end apart: 3 -> 3, of which waited for: 1 -> 1; matrix products, arithmetic and copies ran while one was open for 71% -> 81% of each run, Pallas kernels for 0% -> 0%
where the time goes in v1:
time: 265 us; the launch traced here: 264 us
  local copies, waits for them, and re-layouts  164 us (62%)
  other arithmetic  51.7 us (20%)
  blocking collectives  26 us (10%)
  between operations  14.4 us (5%)
  starting transfers between devices  3.91 us (1%)
    gather x3, local copies, waits for them, and re-layouts, apply_mass(): gathered = jnp.take(flat_ext, tile_slot.reshape(-1), axis=1)  156 us
    all_gather x1, blocking collectives, body(): summed_gram = jnp.sum(lax.all_gather(block_terms, 'dom'), axis=0)  26 us
    select_n x2, other arithmetic, apply_mass(): gathered = jnp.take(flat_ext, tile_slot.reshape(-1), axis=1)  21.3 us
    reduce_sum x2, other arithmetic, apply_mass(): total_sum = total_sum + jnp.sum(tile_part[None] * values[:, None], axis=2)  13.8 us
    mul x1, other arithmetic, apply_mass(): total_sum = total_sum + jnp.sum(tile_part[None] * values[:, None], axis=2)  9.23 us
  transfers between devices with their start and end apart: 3, of which 1 were waited for; matrix products, arithmetic and copies ran while one was open for 81% of the time, Pallas kernels for 0%

profile of v1, /device:TPU:0, one launch (start us, length us, event | category | flops | bytes accessed | tf_op | source)
XLA Modules:
  0.0 263.7 jit_solution(13671890788853013112)
XLA Ops:
  7.2 0.7 all-gather.3.cloned.1.call-update
  7.9 1.8 copy.30
  9.7 0.7 compare_select_fusion.3
  10.4 0.7 compare_and_fusion.2
  11.1 0.7 reshape.93
  11.8 0.5 copy.33
  12.3 2.0 gather_fusion.1
  14.3 0.8 select_bitcast_fusion.1
  15.2 2.4 collective-permute-start
  17.6 2.0 gather_fusion.2
  19.6 0.1 select_bitcast_fusion
  19.7 1.5 collective-permute-start.1
  21.2 1.1 convert_bitcast_fusion.2
  22.3 1.2 bitcast_convert_fusion.2
  23.6 0.1 copy.40
  23.8 0.1 compare_select_fusion
  24.1 0.7 copy-done.10
  24.8 0.4 collective-permute-done.1
  25.2 1.2 pad_maximum_fusion
  26.5 120.6 %gather_fusion = bf16[30720,192]{1,0:T(8,128)(2,1)} fusion(bf16[192,3072]{0,1:T(8,128)(2,1)S(1)} %pad_maximum_fusion, s32[30720]{0:T(1024)S(1)} %broadcast_clamp_fusion), kind=kCustom, calls=%fused_computation.2 | custom fusion | bytes 23715840 | tf_op jit(solution)/shard_map/jit(_take)/gather | solution.py:27
  147.1 18.1 %copy.34 = bf16[192,30720]{1,0:T(8,128)(2,1)} copy(bf16[192,30720]{0,1:T(8,128)(2,1)} %bitcast.70) | data formatting | bytes 23592960 | tf_op jit(solution)/shard_map/jit(_take)/gather | solution.py:27
  165.1 17.4 %gather.10 = bf16[64,3,15,2048]{3,2,1,0:T(8,128)(2,1)} reshape(bf16[192,30720]{1,0:T(8,128)(2,1)} %copy.34) | data formatting | bytes 23592960 | tf_op jit(solution)/shard_map/jit(_take)/gather | solution.py:27
  182.6 21.2 %copy_select_fusion = bf16[64,3,15,2048]{3,0,2,1:T(8,128)(2,1)S(1)} fusion(bf16[64,3,15,2048]{3,2,1,0:T(8,128)(2,1)} %gather.10, pred[15,2048]{1,0:T(8,128)(4,1)S(1)} %compare_and_fusion), kind=kLoop, calls=%fused_computation.6 | loop fusion | flops 5898240 | bytes 23623680 | tf_op jit(solution)/shard_map/jit(_take)/select_n | solution.py:27
  203.8 9.2 %fusion.2 = (f32[64,15,2048]{2,0,1:T(8,128)}, f32[64,15,2048]{2,0,1:T(8,128)}, f32[64,15,2048]{2,0,1:T(8,128)}) fusion(bf16[64,3,15,2048]{3,0,2,1:T(8,128)(2,1)S(1)} %copy_select_fusion), kind=kLoop, calls=%fused_computation.12 | loop fusion | flops 5898240 | bytes 35389440 | tf_op jit(solution)/shard_map/mul | solution.py:32
  213.0 5.1 %multiply_reduce_fusion.2 = f32[64,3,2048]{2,0,1:T(8,128)S(1)} fusion(f32[64,15,2048]{2,0,1:T(8,128)} %get-tuple-element.3, f32[3,15,2048]{2,1,0:T(8,128)S(1)} %copy-done.5), kind=kLoop, calls=%fused_computation.5 | loop fusion | flops 11403264 | bytes 9805824 | tf_op jit(solution)/shard_map/reduce_sum | solution.py:32
  218.2 8.7 %multiply_reduce_fusion = (f32[64,3,2048]{2,0,1:T(8,128)S(1)}, f32[64,3,2048]{2,0,1:T(8,128)S(1)}) fusion(f32[64,15,2048]{2,0,1:T(8,128)} %get-tuple-element.4, f32[3,15,2048]{2,1,0:T(8,128)S(1)} %copy-done.6, f32[64,15,2048]{2,0,1:T(8,128)} %get-tuple-element.5, f32[3,15,2048]{2,1,0:T(8,128)S(1)} %copy-done.7), kind=kLoop, calls=%fused_computation.3 | loop fusion | flops 22806528 | bytes 19611648 | tf_op jit(solution)/shard_map/reduce_sum | solution.py:32
  226.9 0.7 add_convert_fusion
  227.6 2.3 convolution_bitcast_fusion
  230.0 26.0 %all-gather = f32[2048,64]{0,1:T(8,128)S(1)} all-gather(f32[128,64]{0,1:T(8,128)S(1)} %convolution_bitcast_fusion), channel_id=2, replica_groups=mesh['dom'=16,'col'=2] {'dom'}, dimensions={0}, use_global_device_ids=true | all-gather | bytes 557056 | tf_op jit(solution)/shard_map/all_gather | solution.py:54
  256.0 0.1 copy.41
  256.1 0.1 bitcast_reduce_fusion
  256.2 0.6 broadcast_multiply_fusion
  (37 shorter events, 0.4 us)
Async XLA Ops:
  7.2 220.5 %all-gather.3.cloned.1.call-start = ((), (), s32[]{:S(2)}) async-start(), calls=%async_computation | async-start | bytes 2359296 | tf_op jit(solution)/shard_map/all_gather | solution.py:53
  9.7 7.9 %copy-start.11 = (s32[512]{0:T(512)S(1)}, s32[512]{0:T(512)}, u32[]{:S(2)}) copy-start(s32[512]{0:T(512)} %param.11) | copy-start | bytes 6148
  11.8 9.4 %copy-start.8 = (bf16[16,3,3,2048]{3,0,2,1:T(8,128)(2,1)S(1)}, bf16[16,3,3,2048]{3,0,2,1:T(8,128)(2,1)}, u32[]{:S(2)}) copy-start(bf16[16,3,3,2048]{3,0,2,1:T(8,128)(2,1)} %param.8) | copy-start | bytes 1769476
  12.3 10.0 %copy-start = (bf16[64,3,2048]{2,0,1:T(8,128)(2,1)S(1)}, bf16[64,3,2048]{2,0,1:T(8,128)(2,1)}, u32[]{:S(2)}) copy-start(bf16[64,3,2048]{2,0,1:T(8,128)(2,1)} %param.7) | copy-start | bytes 2359300
  15.2 8.9 %collective-permute-start = (bf16[192,512]{0,1:T(8,128)(2,1)}, bf16[192,512]{0,1:T(8,128)(2,1)S(1)}, u32[]{:S(2)}, u32[]{:S(2)}) collective-permute-start(bf16[192,512]{0,1:T(8,128)(2,1)} %select_bitcast_fusion.1), channel_id=1, source_target_pairs={{0,2},{2,4},{4,6},{6,8},{8,10},{10,12},{12,14},{14,16},{16,18},{18... | collective-permute-start | bytes 589832 | tf_op jit(solution)/shard_map/ppermute | solution.py:10
  17.6 6.0 %copy-start.9 = (s32[15,2048]{1,0:T(8,128)S(1)}, s32[15,2048]{1,0:T(8,128)}, u32[]{:S(2)}) copy-start(s32[15,2048]{1,0:T(8,128)} %param.9) | copy-start | bytes 368644
  19.7 5.5 %collective-permute-start.1 = (bf16[192,512]{0,1:T(8,128)(2,1)S(1)}, bf16[192,512]{0,1:T(8,128)(2,1)S(1)}, u32[]{:S(2)}, u32[]{:S(2)}) collective-permute-start(bf16[192,512]{0,1:T(8,128)(2,1)S(1)} %select_bitcast_fusion), channel_id=1, source_target_pairs={{2,0},{4,2},{6,4},{8,6},{10,8},{12,10},{14,12},{16,14},{18,16},{20... | collective-permute-start | bytes 589832 | tf_op jit(solution)/shard_map/ppermute | solution.py:10
  24.1 0.7 copy-start.10
  203.8 9.2 %copy-start.5 = (f32[3,15,2048]{2,1,0:T(8,128)S(1)}, f32[3,15,2048]{2,1,0:T(8,128)}, u32[]{:S(2)}) copy-start(f32[3,15,2048]{2,1,0:T(8,128)} %get-tuple-element.9) | copy-start | bytes 1105924
  213.0 5.1 %copy-start.6 = (f32[3,15,2048]{2,1,0:T(8,128)S(1)}, f32[3,15,2048]{2,1,0:T(8,128)}, u32[]{:S(2)}) copy-start(f32[3,15,2048]{2,1,0:T(8,128)} %get-tuple-element.10) | copy-start | bytes 1105924
  213.0 5.1 %copy-start.7 = (f32[3,15,2048]{2,1,0:T(8,128)S(1)}, f32[3,15,2048]{2,1,0:T(8,128)}, u32[]{:S(2)}) copy-start(f32[3,15,2048]{2,1,0:T(8,128)} %get-tuple-element.11) | copy-start | bytes 1105924
  218.1 8.7 %copy-start.2 = (f32[64,2048]{1,0:T(8,128)S(1)}, f32[64,2048]{1,0:T(8,128)}, u32[]{:S(2)}) copy-start(f32[64,2048]{1,0:T(8,128)} %get-tuple-element.6) | copy-start | bytes 1572868
  218.1 8.7 %copy-start.3 = (f32[64,2048]{1,0:T(8,128)S(1)}, f32[64,2048]{1,0:T(8,128)}, u32[]{:S(2)}) copy-start(f32[64,2048]{1,0:T(8,128)} %get-tuple-element.7) | copy-start | bytes 1572868
  218.1 8.7 %copy-start.4 = (f32[64,2048]{1,0:T(8,128)S(1)}, f32[64,2048]{1,0:T(8,128)}, u32[]{:S(2)}) copy-start(f32[64,2048]{1,0:T(8,128)} %get-tuple-element.8) | copy-start | bytes 1572868
  227.6 29.2 %copy-start.1 = (bf16[64,3,2048]{2,0,1:T(8,128)(2,1)}, bf16[64,3,2048]{2,0,1:T(8,128)(2,1)S(1)}, u32[]{:S(2)}) copy-start(bf16[64,3,2048]{2,0,1:T(8,128)(2,1)S(1)} %add_convert_fusion) | copy-start | bytes 2359300
Sparse Core Ops, SparseCore 0:
  9.5 29.8 all-gather.2
